TPU v7x, 128 devices: a whole 4x4x4 slice. The times are simulated.
128 devices in a mesh: dp: 16 (over y_lo, x, core), tensor: 8 (over y_hi, z).
Axes of the slice: x: 4, y: 4 (y_hi: 2, y_lo: 2; y = y_hi * 2 + y_lo), z: 4, core: 2. Of those that a mesh axis runs over, the one named last changes fastest.
Arguments:
- context: bfloat16 [2048, 180, 768], P(('dp', 'tensor')), may hold values from -6 to 6
- stream: bfloat16 [2048, 180, 768], P(('dp', 'tensor')), may hold values from -6 to 6
- out_weight: bfloat16 [768, 768], replicated, may hold values from -0.21875 to 0.21875
- gain: float32 [768], replicated, may hold values from 0.5 to 1.5
- bias: float32 [768], replicated, may hold values from -3 to 3
- proj_weight: bfloat16 [768, 128], replicated, may hold values from -0.21875 to 0.21875
- query_states: bfloat16 [32, 32, 768], P('dp'), may hold values from -6 to 6
- passage_len: int32 [2048], P(('dp', 'tensor')), may hold values from 45 to 180, as said below
- passage_dest: int32 [2048], P(('dp', 'tensor')), may hold values from 0 to 2047, as said below
- teacher_states: bfloat16 [2048, 212, 1024], P(('dp', 'tensor')), may hold values from -6 to 6
- teacher_query: bfloat16 [1024, 1024], P(None, 'tensor'), may hold values from -0.1875 to 0.1875
- teacher_key: bfloat16 [1024, 1024], P(None, 'tensor'), may hold values from -0.1875 to 0.1875
Outputs:
- loss: float32 [], replicated
- grad_out: float32 [768, 768], replicated
- grad_proj: float32 [768, 128], replicated
- grad_gain: float32 [768], replicated
- grad_bias: float32 [768], replicated
- grad_context: bfloat16 [2048, 180, 768], P(('dp', 'tensor'))
Inputs may be any that keep to these rules, and one draw needn't show every extreme that they name: `passage_dest`: A permutation of the pair positions. Passage rows form runs of 16 (run a = i * 8 + t), and so do pair positions; run a sends exactly 16 / 16 of its rows into each pair run j * 8 + t, for every j. `passage_len`: every run of 16 passage rows holds one passage of full length.
All inputs are finite; a program needn't handle non-finite values.
Results may differ from a plain program's by a relative error of at most 0.011.
Values may be sent and summed in bfloat16 or wider, within the bound.
A program may use at most 192 MiB of HBM per device.

v0:
```python
import math

import jax
import jax.numpy as jnp
from jax import lax
from jax.sharding import PartitionSpec as P

NPQ = 64
TD = 1024


sharpness_divisor = 0.05
softcap = 10.0
epsilon = 1e-06


def token_scores(
    matched_search_rescaled,
    matched_direction_arrays,
    pair_len,
    teacher,
    search_word_entries,
    seq_len,
):
    learner_raw_ratings = (
        jnp.einsum(
            "hsn,hfn->hsf",
            matched_search_rescaled,
            matched_direction_arrays,
            preferred_element_type=jnp.float32,
        )
        / sharpness_divisor
    )
    valid = jnp.arange(seq_len, dtype=jnp.int32)[None, None, :] < pair_len[:, None, None]
    student_exp = jnp.where(valid, jnp.exp(learner_raw_ratings), 0.0)
    student_total = jnp.sum(student_exp, axis=-1, keepdims=True)
    learner_likelihood = student_exp / student_total
    student_log = learner_raw_ratings - jnp.log(student_total)
    teacher_exp = jnp.where(valid, jnp.exp(teacher), 0.0)
    teacher_total = jnp.sum(teacher_exp, axis=-1, keepdims=True)
    mentor_likelihood = teacher_exp / teacher_total
    teacher_log = teacher - jnp.log(teacher_total)
    diverge = jnp.sum(
        jnp.where(valid, mentor_likelihood * (teacher_log - student_log), 0.0), axis=-1
    )
    loss_part = jnp.sum(diverge)
    angle_similarity_slope = (
        (learner_likelihood - mentor_likelihood) / (search_word_entries * sharpness_divisor)
    ).astype(jnp.bfloat16)
    unit_grad = jnp.einsum(
        "pqk,pqc->pkc",
        angle_similarity_slope,
        matched_search_rescaled,
        preferred_element_type=jnp.float32,
    ).astype(jnp.bfloat16)
    pair_qgrad = jnp.einsum(
        "pqk,pkc->pqc",
        angle_similarity_slope,
        matched_direction_arrays,
        preferred_element_type=jnp.float32,
    )
    return (loss_part, unit_grad, pair_qgrad)


def local(
    context,
    stream,
    out_weight,
    gain,
    bias,
    proj_weight,
    query_states,
    passage_len,
    passage_dest,
    teacher_states,
    teacher_query,
    teacher_key,
):
    dp_count = lax.axis_size("dp")
    tensor_count = lax.axis_size("tensor")
    pair_count, seq_len, width = context.shape
    search_word_entries = query_states.shape[1]
    per_dest = pair_count // dp_count
    summed = stream.astype(jnp.float32) + jnp.einsum(
        "ptd,de->pte", context, out_weight, preferred_element_type=jnp.float32
    )
    centred = summed - jnp.mean(summed, axis=-1, keepdims=True)
    inverse = lax.rsqrt(jnp.mean(centred * centred, axis=-1, keepdims=True) + epsilon)
    normed = centred * inverse
    hidden = (normed * gain + bias).astype(jnp.bfloat16)
    embeds = jnp.einsum("ptd,de->pte", hidden, proj_weight, preferred_element_type=jnp.float32)
    length = jnp.sqrt(jnp.sum(embeds * embeds, axis=-1, keepdims=True) + epsilon)
    direction = embeds / length
    unit_vecs = direction.astype(jnp.bfloat16)
    dest_group = passage_dest // (pair_count * tensor_count)
    send_order = jnp.argsort(dest_group, stable=True)
    restore = jnp.argsort(send_order)
    scale = 1.0 / math.sqrt(TD)
    piece = lax.all_gather(teacher_states, "tensor", axis=0, tiled=True)
    query_side = jnp.einsum(
        "pqd,de->pqe",
        piece[:, :search_word_entries],
        teacher_query,
        preferred_element_type=jnp.float32,
    ).astype(jnp.bfloat16)
    key_side = jnp.einsum(
        "pkd,de->pke",
        piece[:, search_word_entries:],
        teacher_key,
        preferred_element_type=jnp.float32,
    ).astype(jnp.bfloat16)
    scores = jnp.einsum("pqe,pke->pqk", query_side, key_side, preferred_element_type=jnp.float32)
    partials = scores.reshape(piece.shape[0], -1) * scale
    raw_map = lax.psum_scatter(partials, "tensor", scatter_dimension=0, tiled=True)
    teacher = (softcap * jnp.tanh(raw_map / softcap)).reshape(
        pair_count, search_word_entries, seq_len
    )
    query_embeds = jnp.einsum(
        "nqd,de->nqe", query_states, proj_weight, preferred_element_type=jnp.float32
    )
    query_length = jnp.sqrt(jnp.sum(query_embeds * query_embeds, axis=-1, keepdims=True) + epsilon)
    query_dir = query_embeds / query_length
    query_unit = query_dir.astype(jnp.bfloat16)
    group_queries = query_states.shape[0]
    send_units = unit_vecs[send_order].reshape(dp_count, per_dest, seq_len, -1)
    send_info = jnp.stack(
        [passage_dest[send_order] % pair_count, passage_len[send_order]], axis=-1
    ).reshape(dp_count, per_dest, 2)
    got_units, got_info = (
        lax.all_to_all(send_units, "dp", split_axis=0, concat_axis=0, tiled=True),
        lax.all_to_all(send_info, "dp", split_axis=0, concat_axis=0, tiled=True),
    )
    got_info = got_info.reshape(pair_count, 2)
    slot_index = got_info[:, 0]
    placing = jnp.argsort(slot_index)
    matched_direction_arrays = got_units.reshape(pair_count, seq_len, -1)[placing]
    pair_len = got_info[:, 1][placing]
    first_pair = lax.axis_index("tensor") * pair_count
    pair_query = (first_pair + jnp.arange(pair_count, dtype=jnp.int32)) // NPQ
    chooser = (pair_query[:, None] == jnp.arange(group_queries, dtype=jnp.int32)[None, :]).astype(
        jnp.bfloat16
    )
    matched_search_rescaled = jnp.einsum(
        "pn,nqc->pqc", chooser, query_unit, preferred_element_type=jnp.float32
    ).astype(jnp.bfloat16)
    loss_part, unit_grad, pair_qgrad = token_scores(
        matched_search_rescaled,
        matched_direction_arrays,
        pair_len,
        teacher,
        search_word_entries,
        seq_len,
    )
    query_grad = jnp.einsum(
        "pn,pqc->nqc", chooser.astype(jnp.float32), pair_qgrad, precision=lax.Precision.HIGHEST
    )
    back_units = unit_grad[slot_index].reshape(dp_count, per_dest, seq_len, -1)
    returned = lax.all_to_all(back_units, "dp", split_axis=0, concat_axis=0, tiled=True).reshape(
        pair_count, seq_len, -1
    )
    upstream = returned[restore].astype(jnp.float32)
    query_embed_grad = (
        query_grad - query_dir * jnp.sum(query_dir * query_grad, axis=-1, keepdims=True)
    ) / query_length
    proj_query = jnp.einsum(
        "nqd,nqe->de",
        query_states.astype(jnp.float32),
        query_embed_grad,
        precision=lax.Precision.HIGHEST,
    )
    embed_grad = (
        (upstream - direction * jnp.sum(direction * upstream, axis=-1, keepdims=True)) / length
    ).astype(jnp.bfloat16)
    proj_grad = (
        jnp.einsum("ptd,pte->de", hidden, embed_grad, preferred_element_type=jnp.float32)
        + proj_query
    )
    hidden_grad = jnp.einsum(
        "pte,de->ptd", embed_grad, proj_weight, preferred_element_type=jnp.float32
    )
    gain_grad = jnp.sum(hidden_grad * normed, axis=(0, 1))
    bias_grad = jnp.sum(hidden_grad, axis=(0, 1))
    scaled = hidden_grad * gain
    summed_grad = (
        inverse
        * (
            scaled
            - jnp.mean(scaled, axis=-1, keepdims=True)
            - normed * jnp.mean(scaled * normed, axis=-1, keepdims=True)
        )
    ).astype(jnp.bfloat16)
    wo_grad = jnp.einsum("ptd,pte->de", context, summed_grad, preferred_element_type=jnp.float32)
    grad_context = jnp.einsum(
        "pte,de->ptd", summed_grad, out_weight, preferred_element_type=jnp.float32
    ).astype(jnp.bfloat16)
    totals = lax.psum((loss_part, wo_grad, proj_grad, gain_grad, bias_grad), ("dp", "tensor"))
    loss = totals[0] / (pair_count * dp_count * tensor_count * search_word_entries)
    return (loss, totals[1], totals[2], totals[3], totals[4], grad_context)


def solution(mesh):
    return jax.shard_map(
        local,
        mesh=mesh,
        in_specs=(
            P(("dp", "tensor"), None, None),
            P(("dp", "tensor"), None, None),
            P(),
            P(),
            P(),
            P(),
            P("dp", None, None),
            P(("dp", "tensor")),
            P(("dp", "tensor")),
            P(("dp", "tensor"), None, None),
            P(None, "tensor"),
            P(None, "tensor"),
        ),
        out_specs=(P(), P(), P(), P(), P(), P(("dp", "tensor"), None, None)),
        check_vma=False,
    )
```

profile of v0, /device:TPU:1, one launch (start us, length us, event | category | flops | bytes accessed | tf_op | source)
XLA Modules:
  0.0 923.3 jit_solution(18118599831477731849)
XLA Ops:
  7.2 0.7 all-gather.2.cloned.1.call-update
  8.0 1.2 sort.48
  9.3 536.0 %all-gather.2.cloned.1.call-done = bf16[128,212,1024]{2,0,1:T(8,128)(2,1)} async-done(((bf16[16,212,1024]{2,0,1:T(8,128)(2,1)}), bf16[128,212,1024]{2,0,1:T(8,128)(2,1)}) %all-gather.2.cloned.1.call-update) | async-done | bytes 55574544 | tf_op jit(solution)/shard_map/all_gather | solution.py:99
  545.3 19.7 %convolution_convert_fusion = bf16[128,180,128]{2,0,1:T(8,128)(2,1)S(1)} fusion(bf16[128,212,1024]{2,0,1:T(8,128)(2,1)} %all-gather.2.cloned.1.call-done, bf16[1024,128]{1,0:T(8,128)(2,1)S(1)} %copy-done.10), kind=kOutput, calls=%fused_computation.24 | convolution fusion | flops 6042746880 | bytes 61734912 | tf_op jit(solution)/shard_map/pkd,de->pke/dot_general | solution.py:106
  565.1 5.7 convolution_convert_fusion.2
  570.8 8.0 fusion.11
  578.8 5.5 reshape.237
  584.3 0.7 gather_fusion
  585.0 0.7 gather_fusion.1
  585.7 0.7 copy.62
  586.4 6.1 all-to-all-start
  592.5 1.2 sort.50
  593.8 0.3 multiply_reduce_fusion.6
  594.0 12.0 %fusion.82 = (f32[16,180]{1,0:T(8,128)S(1)}, f32[16,180,768]{2,1,0:T(8,128)S(1)}) fusion(bf16[768,768]{1,0:T(8,128)(2,1)S(1)} %copy-done, bf16[16,180,768]{2,0,1:T(8,128)(2,1)} %param.12, bf16[16,180,768]{2,0,1:T(8,128)(2,1)} %param.13), kind=kOutput, calls=%fused_computation.134 | convolution fusion | flops 3404018944 | bytes 18885888 | tf_op jit(solution)/shard_map/ptd,de->pte/dot_general | solution.py:84
  606.1 1.3 multiply_reduce_fusion.2
  607.4 2.1 copy-done.3
  609.5 2.3 multiply_reduce_fusion.4
  612.2 0.8 copy-done.5
  613.0 0.5 fusion.81
  613.5 1.5 gather_fusion.3
  615.0 15.8 %all-to-all-start.1 = ((bf16[16,1,180,128]{3,2,1,0:T(8,128)(2,1)}), bf16[16,1,180,128]{3,2,1,0:T(8,128)(2,1)S(1)}, u32[]{:S(2)}, u32[]{:S(2)}) async-start(bf16[16,1,180,128]{3,2,1,0:T(8,128)(2,1)} %bitcast.12), calls=%async_computation.1 | async-start | bytes 1507328 | tf_op jit(solution)/shard_map/all_to_all | solution.py:130
  630.9 1.2 sort.49
  632.1 0.7 gather_fusion.2
  632.9 10.2 %all-to-all-done.1 = bf16[16,1,180,128]{3,2,1,0:T(8,128)(2,1)S(1)} async-done(((bf16[16,1,180,128]{3,2,1,0:T(8,128)(2,1)}), bf16[16,1,180,128]{3,2,1,0:T(8,128)(2,1)S(1)}, u32[]{:S(2)}, u32[]{:S(2)}) %all-to-all-start.1) | async-done | bytes 737312 | tf_op jit(solution)/shard_map/all_to_all | solution.py:130
  643.1 0.7 gather_fusion.4
  643.8 24.6 %reduce-scatter.4.cloned.1.call-done = f32[16,5760]{1,0:T(8,128)} async-done(((f32[128,5760]{1,0:T(8,128)}), f32[16,5760]{1,0:T(8,128)}) %reduce-scatter.4.cloned.1.call-update) | async-done | bytes 368656 | tf_op jit(solution)/shard_map/reduce_scatter | solution.py:114
  668.4 1.0 tanh_multiply_fusion
  669.5 0.7 reshape.161
  670.2 0.7 fusion.33
  670.9 2.4 select_reduce_fusion
  673.3 1.9 convolution_convert_fusion.3
  675.3 1.5 gather_fusion.5
  676.8 6.3 all-to-all-start.2
  683.2 2.2 fusion.27
  685.4 1.3 fusion.37
  686.9 8.6 all-to-all-done.2
  695.5 0.7 gather_fusion.6
  696.2 23.3 %multiply_reduce_fusion = (f32[768]{0:T(1024)S(1)}, f32[16,180]{1,0:T(8,128)S(1)}, f32[16,180]{1,0:T(8,128)S(1)}, f32[768]{0:T(1024)S(1)}, f32[16,180,768]{2,1,0:T(8,128)}) fusion(f32[16,180,768]{2,1,0:T(8,128)} %copy-done.3, f32[16,180]{1,0:T(8,128)S(1)} %add_rsqrt_fusion, f32[16,180]{1,0:T(8,128)S(1)} %broadcast_multiply_fusion.2, f32[768]{0:T(1024)S(1)} %copy-done.9, ...), kind=kOutput, calls=%fused_computation.10 | convolution fusion | flops 589451072 | bytes 20169984 | tf_op jit(solution)/shard_map/pte,de->ptd/dot_general | solution.py:178
  719.4 23.2 %convolution_bitcast_fusion.1 = f32[768,128]{1,0:T(8,128)S(1)} fusion(bf16[16,180,128]{2,1,0:T(8,128)(2,1)S(1)} %gather_fusion.6, f32[16,180]{1,0:T(8,128)S(1)} %add_sqrt_fusion, f32[16,180,768]{2,1,0:T(8,128)} %copy-done.3, f32[768]{0:T(1024)S(1)} %copy-done.12, f32[768]{0:T(1024)S(1)} %copy-done.9, f32[16,180]{1,0:T(8,128)S(1)} %add_rsqrt_fusion, ...), kind=kOutput, calls=%fused_computation.42 | convolution fusion | flops 580611008 | bytes 11493120 | tf_op jit(solution)/shard_map/ptd,pte->de/dot_general | solution.py:175
  742.7 7.5 multiply_convert_fusion
  750.2 9.7 %fusion.14 = f32[768,768]{0,1:T(8,128)} fusion(bf16[16,180,768]{2,1,0:T(8,128)(2,1)S(1)} %multiply_convert_fusion, bf16[16,180,768]{2,0,1:T(8,128)(2,1)} %param.12), kind=kOutput, calls=%fused_computation.29 | convolution fusion | flops 3397386240 | bytes 11206656 | tf_op jit(solution)/shard_map/ptd,pte->de/dot_general | solution.py:192
  760.0 1.1 fusion.24
  761.1 65.1 %all-reduce = (f32[]{:T(128)}, f32[768]{0:T(1024)}, f32[768]{0:T(1024)}) all-reduce(f32[]{:T(128)} %get-tuple-element.57, f32[768]{0:T(1024)S(1)} %get-tuple-element.36, f32[768]{0:T(1024)S(1)} %get-tuple-element.39), channel_id=1, replica_groups=mesh['dp'=16,'tensor'=8] {'dp','tensor'}, use_global_device_ids=true, to_apply=%region_10.11 | all-reduce | flops 1537 | bytes 12296 | tf_op jit(solution)/shard_map/psum | solution.py:196
  826.3 6.0 convolution_convert_fusion.1
  832.3 2.9 copy.81
  835.9 75.7 %all-reduce.4.cloned.1.call-done = (f32[768,768]{0,1:T(8,128)}, f32[768,128]{1,0:T(8,128)}) async-done(((f32[768,768]{0,1:T(8,128)}, f32[768,128]{1,0:T(8,128)}), (f32[768,768]{0,1:T(8,128)}, f32[768,128]{1,0:T(8,128)})) %all-reduce.4.cloned.1.call-update) | async-done | bytes 2752528 | tf_op jit(solution)/shard_map/psum | solution.py:196
  911.6 3.1 copy.80
  914.7 0.7 copy.121
  (57 shorter events, 1.0 us)
Async XLA Ops:
  7.2 586.9 %copy-start = (bf16[768,768]{1,0:T(8,128)(2,1)S(1)}, bf16[768,768]{1,0:T(8,128)(2,1)}, u32[]{:S(2)}) copy-start(bf16[768,768]{1,0:T(8,128)(2,1)} %param.14) | copy-start | bytes 3538948
  7.2 0.8 copy-start.1
  7.2 538.1 %copy-start.10 = (bf16[1024,128]{1,0:T(8,128)(2,1)S(1)}, bf16[1024,128]{1,0:T(8,128)(2,1)}, u32[]{:S(2)}) copy-start(bf16[1024,128]{1,0:T(8,128)(2,1)} %param.23) | copy-start | bytes 786436
  7.2 538.1 %all-gather.2.cloned.1.call-start = ((), (), s32[]{:S(2)}) async-start(), calls=%async_computation.4 | async-start | bytes 62521344 | tf_op jit(solution)/shard_map/all_gather | solution.py:99
  7.9 660.5 %reduce-scatter.4.cloned.1.call-start = ((), (), s32[]{:S(2)}) async-start(), calls=%async_computation.5 | async-start | bytes 3317760 | tf_op jit(solution)/shard_map/reduce_scatter | solution.py:114
  9.3 555.8 %copy-start.11 = (bf16[1024,128]{1,0:T(8,128)(2,1)S(1)}, bf16[1024,128]{1,0:T(8,128)(2,1)}, u32[]{:S(2)}) copy-start(bf16[1024,128]{1,0:T(8,128)(2,1)} %param.22) | copy-start | bytes 786436
  578.8 6.2 copy-start.2
  578.8 14.9 %copy-start.7 = (bf16[2,32,768]{2,1,0:T(8,128)(2,1)S(1)}, bf16[2,32,768]{2,1,0:T(8,128)(2,1)}, u32[]{:S(2)}) copy-start(bf16[2,32,768]{2,1,0:T(8,128)(2,1)} %param.18) | copy-start | bytes 294916
  578.8 14.9 %copy-start.8 = (bf16[768,128]{1,0:T(8,128)(2,1)S(1)}, bf16[768,128]{1,0:T(8,128)(2,1)}, u32[]{:S(2)}) copy-start(bf16[768,128]{1,0:T(8,128)(2,1)} %param.17) | copy-start | bytes 589828
  586.4 28.6 %all-to-all-start = ((s32[16,1,2]{2,1,0:T(1,128)}), s32[16,1,2]{2,1,0:T(1,128)S(1)}, u32[]{:S(2)}, u32[]{:S(2)}) async-start(s32[16,1,2]{2,1,0:T(1,128)} %copy.62), calls=%async_computation | async-start | bytes 16384 | tf_op jit(solution)/shard_map/all_to_all | solution.py:131
  606.0 3.5 copy-start.3
  606.1 3.5 copy-start.9
  606.1 3.5 copy-start.12
  611.9 1.1 copy-start.5
  615.0 28.1 %all-to-all-start.1 = ((bf16[16,1,180,128]{3,2,1,0:T(8,128)(2,1)}), bf16[16,1,180,128]{3,2,1,0:T(8,128)(2,1)S(1)}, u32[]{:S(2)}, u32[]{:S(2)}) async-start(bf16[16,1,180,128]{3,2,1,0:T(8,128)(2,1)} %bitcast.12), calls=%async_computation.1 | async-start | bytes 1507328 | tf_op jit(solution)/shard_map/all_to_all | solution.py:130
  676.8 18.7 %all-to-all-start.2 = ((bf16[16,1,180,128]{3,2,1,0:T(8,128)(2,1)}), bf16[16,1,180,128]{3,2,1,0:T(8,128)(2,1)S(1)}, u32[]{:S(2)}, u32[]{:S(2)}) async-start(bf16[16,1,180,128]{3,2,1,0:T(8,128)(2,1)} %bitcast.16), calls=%async_computation.2 | async-start | bytes 1507328 | tf_op jit(solution)/shard_map/all_to_all | solution.py:158
  683.1 228.4 %all-reduce.4.cloned.1.call-start = ((), (), s32[]{:S(2)}) async-start(), calls=%async_computation.6 | async-start | bytes 5505024 | tf_op jit(solution)/shard_map/psum | solution.py:196
  750.2 9.8 %copy-start.4 = (bf16[16,180,768]{2,1,0:T(8,128)(2,1)}, bf16[16,180,768]{2,1,0:T(8,128)(2,1)S(1)}, u32[]{:S(2)}) copy-start(bf16[16,180,768]{2,1,0:T(8,128)(2,1)S(1)} %multiply_convert_fusion) | copy-start | bytes 13271044
  911.6 3.1 copy-start.6
Sparse Core Ops, SparseCore 0:
  10.4 534.8 all-gather.1
  584.4 83.9 reduce-scatter.3
  761.3 150.2 all-reduce.3
where the time goes:
time: 928 us; the launch traced here: 923 us
  waiting for transfers between devices  656 us (71%)
  matrix products  118 us (13%)
  blocking collectives  65.1 us (7%)
  starting transfers between devices  28.3 us (3%)
  local copies, waits for them, and re-layouts  23.1 us (2%)
  other arithmetic  17 us (2%)
  between operations  16.1 us (2%)
    all_gather x1, waiting for transfers between devices, local(): piece = lax.all_gather(teacher_states, 'tensor', axis=0, tiled=True)  536 us
    psum x1, waiting for transfers between devices, local(): lax.psum((loss_part, wo_grad, proj_grad, gain_grad, bias_grad), ('dp', 't...  75.7 us
    psum x1, blocking collectives, local(): lax.psum((loss_part, wo_grad, proj_grad, gain_grad, bias_grad), ('dp', 't...  65.1 us
    reduce_scatter x1, waiting for transfers between devices, local(): lax.psum_scatter(partials, 'tensor', scatter_dimension=0, tiled=True)  24.6 us
    dot_general x1, matrix products, local(): jnp.einsum('pte,de->ptd', embed_grad, proj_weight, preferred_element_type...  23.3 us
    dot_general x1, matrix products, local(): jnp.einsum('ptd,pte->de', hidden, embed_grad, preferred_element_type=jnp....  23.2 us
    dot_general x1, matrix products, local(): jnp.einsum('pkd,de->pke', piece[:, search_word_entries:], teacher_key, pr...  19.7 us
  transfers between devices with their start and end apart: 6, of which 5 were waited for; matrix products, arithmetic and copies ran while one was open for 4% of the time, Pallas kernels for 0%

commit v1 on v0

v1 whole, which is shorter than its diff:
```python
import jax
import jax.numpy as jnp
from jax import lax
from jax.experimental import pallas as pl
from jax.experimental.pallas import tpu as pltpu
from jax.sharding import PartitionSpec as P

MESH = pl.DeviceIdType.MESH
F32, BF16 = jnp.float32, jnp.bfloat16
EPS = 1e-06
SHARP = 0.05
CAP = 10.0

PD = 16
LP = 180
ROW = 192
D = 768
EMB = 128
TD = 1024
QW = 32
ND, NT = 16, 8
FLAT = PD * ROW
NN = (((1,), (0,)), ((), ()))
NT_DIMS = (((1,), (1,)), ((), ()))
TN_DIMS = (((0,), (0,)), ((), ()))


def mm(a, b, dims=NN):
    return lax.dot_general(a, b, dims, preferred_element_type=F32)


def mm_exact(a, b):
    return lax.dot_general(
        a, b, NN, precision=lax.Precision.HIGHEST, preferred_element_type=F32
    )


def kernel(
    dest_s, len_s, ctx_h, str_h, ts_h, wo, gain, bias, proj, qs, dest_v, wq_h, wk_h,
    gc_h, res_o, gb_o, loss_o,
    ctx_v, str_v, ts_v, c2d, n2d, sg2d, e_s, ee_s, inv_s, il_s, ug, u16,
    wq, wk, maps, stage, rmaps, qbuf, qd_s, qil_s, dinfo, slot_v, slot_s, qgs, qgr, ltb,
    pq_s, cs_s, xq, qm, tm, ar, r0, w1, r1, w2, r2, w3, r3, res,
    sem_in, sem_ts, sem_w, sem_slot, sem_out, sem_a, sem_b, sem_c, sem_d, sem_e, sem_l, sem_g,
):
    dp, tn = lax.axis_index("dp"), lax.axis_index("tensor")
    ylo, x, core = dp // 8, (dp // 2) % 4, dp % 2
    yhi, z = tn // 4, tn % 4
    y = yhi * 2 + ylo

    def dev(y_, x_, core_, z_):
        return ((y_ % 2) * 8 + x_ * 2 + core_, (y_ // 2) * 4 + z_)

    def on_axis(axis, d):
        if axis == "x":
            return dev(y, (x + d) % 4, core, z)
        if axis == "y":
            return dev((y + d) % 4, x, core, z)
        return dev(y, x, core, (z + d) % 4)

    sibling = dev(y, x, 1 - core, z)
    cross = ((dp + 8) % ND, (tn + 4) % NT)

    def fetch_p(p):
        return (
            pltpu.make_async_copy(ctx_h.at[p], ctx_v.at[p], sem_in.at[0, p]),
            pltpu.make_async_copy(str_h.at[p], str_v.at[p], sem_in.at[1, p]),
        )

    def fetch_t(p):
        return pltpu.make_async_copy(ts_h.at[p], ts_v.at[p], sem_ts.at[p])

    @pl.loop(0, PD)
    def _(p):
        for c in fetch_p(p):
            c.start()

    own_w = [
        pltpu.make_async_copy(wq_h, wq.at[tn], sem_w.at[0]),
        pltpu.make_async_copy(wk_h, wk.at[tn], sem_w.at[1]),
    ]
    for c in own_w:
        c.start()

    peers = [((dp + d) % ND, tn) for d in range(1, ND)]
    peers += [(dp, (tn + d) % NT) for d in range(1, NT)]
    peers += [cross]
    barrier = pltpu.get_barrier_semaphore()
    for peer in peers:
        pl.semaphore_signal(barrier, inc=1, device_id=peer, device_id_type=MESH)

    q_in = qs[yhi]
    q_emb = mm(q_in, proj[...])
    q_il = lax.rsqrt(jnp.sum(q_emb * q_emb, axis=-1, keepdims=True) + EPS)
    q_dir = q_emb * q_il
    qd_s[...] = q_dir
    qil_s[...] = jnp.broadcast_to(q_il, (QW, EMB))
    qbuf[dp] = q_dir.astype(BF16)
    dinfo[dp] = dest_v[...]
    maps[...] = jnp.zeros((PD, QW, 256), BF16)

    @pl.loop(0, PD)
    def _(p):
        r = pl.multiple_of(p * ROW + 176, 16)
        for ref in (c2d, n2d, sg2d):
            ref[pl.ds(r, 16), :] = jnp.zeros((16, D), BF16)
        ee_s[pl.ds(r, 16), :] = jnp.zeros((16, EMB), BF16)

    for c in own_w:
        c.wait()
    pl.semaphore_wait(barrier, len(peers))

    started = []

    def rcopy(src, dst, sem, k, to):
        return pltpu.make_async_remote_copy(
            src_ref=src, dst_ref=dst, send_sem=sem.at[0, k], recv_sem=sem.at[1, k],
            device_id=to, device_id_type=MESH,
        )

    def go(copy):
        copy.start()
        started.append(copy)

    def send_all(buf, sem):
        out = []
        for d in range(1, ND):
            c = rcopy(buf.at[dp], buf.at[dp], sem, d - 1, ((dp + d) % ND, tn))
            go(c)
            out.append(c)
        return out

    dcopies = send_all(dinfo, sem_a)
    half = TD // 2
    base = core * half
    wcopies = {}
    counter = [0]

    def rows_of(part):
        if part == "all":
            return base, half
        if part == "hi":
            return base, half // 2
        return base + half // 2, half // 2

    def wsend(name, buf, t_, part, to):
        start, size = rows_of(part)
        view = buf.at[t_, pl.ds(pl.multiple_of(start, 16), size)]
        c = rcopy(view, view, sem_b, counter[0], to)
        counter[0] += 1
        go(c)
        wcopies[name] = c

    zp, zm = on_axis("z", 1), on_axis("z", 3)
    t_zm, t_zp, t_zz = yhi * 4 + (z + 3) % 4, yhi * 4 + (z + 1) % 4, yhi * 4 + (z + 2) % 4

    def flip(t_):
        return (t_ + 4) % NT

    wsend("q_x", wq, tn, "all", cross)
    wsend("q_zp", wq, tn, "all", zp)
    wsend("q_zm", wq, tn, "all", zm)
    wsend("k_zp", wk, tn, "all", zp)
    wsend("k_zm", wk, tn, "all", zm)
    wsend("k_x", wk, tn, "all", cross)
    qcopies = send_all(qbuf, sem_c)

    def got(*names):
        for n in names:
            wcopies[n].wait_recv()

    def step2q():
        got("q_zp", "q_zm", "q_x")
        wsend("q_x_zp", wq, flip(tn), "all", zp)
        wsend("q_x_zm", wq, flip(tn), "all", zm)
        wsend("q_zz_p", wq, t_zm, "hi", zp)
        wsend("q_zz_m", wq, t_zp, "lo", zm)
        wsend("s_q_zm", wq, t_zm, "all", sibling)
        wsend("s_q_zp", wq, t_zp, "all", sibling)
        wsend("s_q_x", wq, flip(tn), "all", sibling)

    def step2k():
        got("k_zp", "k_zm", "k_x")
        wsend("k_zm_x", wk, t_zm, "all", cross)
        wsend("k_zp_x", wk, t_zp, "all", cross)
        wsend("k_zz_p", wk, t_zm, "hi", zp)
        wsend("k_zz_m", wk, t_zp, "lo", zm)
        wsend("s_k_zm", wk, t_zm, "all", sibling)
        wsend("s_k_zp", wk, t_zp, "all", sibling)
        wsend("s_k_x", wk, flip(tn), "all", sibling)

    def step3():
        got("q_x_zp", "q_x_zm")
        wsend("q_xzz_p", wq, flip(t_zm), "hi", zp)
        wsend("q_xzz_m", wq, flip(t_zp), "lo", zm)
        wsend("s_q_xzm", wq, flip(t_zm), "all", sibling)
        wsend("s_q_xzp", wq, flip(t_zp), "all", sibling)
        got("q_zz_p", "q_zz_m")
        wsend("s_q_zz", wq, t_zz, "all", sibling)
        got("k_zz_p", "k_zz_m")
        wsend("k_zz_x", wk, t_zz, "all", cross)
        wsend("s_k_zz", wk, t_zz, "all", sibling)

    def step4():
        got("q_xzz_p", "q_xzz_m")
        wsend("s_q_xzz", wq, flip(t_zz), "all", sibling)
        got("k_zm_x", "k_zp_x")
        wsend("s_k_xzm", wk, flip(t_zm), "all", sibling)
        wsend("s_k_xzp", wk, flip(t_zp), "all", sibling)
        got("k_zz_x")
        wsend("s_k_xzz", wk, flip(t_zz), "all", sibling)

    def forward(ps):
        for p in ps:
            for c in fetch_p(p):
                c.wait()
        xs = [ctx_v[p] for p in ps]
        ss = [mm(v, wo[...]) for v in xs]
        for p, v, s in zip(ps, xs, ss):
            row = pl.ds(pl.multiple_of(p * ROW, 16), LP)
            s = s + str_v[p].astype(F32)
            c = s - jnp.mean(s, axis=-1, keepdims=True)
            inv = lax.rsqrt(jnp.mean(c * c, axis=-1, keepdims=True) + EPS)
            n = c * inv
            h = (n * gain[...] + bias[...]).astype(BF16)
            e = mm(h, proj[...])
            il = lax.rsqrt(jnp.sum(e * e, axis=-1, keepdims=True) + EPS)
            c2d[row, :] = v
            n2d[row, :] = n.astype(BF16)
            inv_s[row, :] = inv
            e_s[row, :] = e
            il_s[row, :] = il
            u16[p] = (e * il).astype(BF16)

    def forward_loop(lo, hi):
        @pl.loop(lo // 2, hi // 2)
        def _(i):
            forward([2 * i, 2 * i + 1])

    @pl.loop(0, PD)
    def _(p):
        fetch_t(p).start()

    forward_loop(0, 6)
    step2q()
    forward_loop(6, 10)
    step2k()
    forward_loop(10, 16)

    for c in dcopies:
        c.wait_recv()
    dest_all = dinfo[:, 0, :]
    lane = lax.broadcasted_iota(jnp.int32, (ND, EMB), 1)
    mine = jnp.logical_and((dest_all // (PD * NT)) == dp, lane < PD)
    slots = jnp.max(jnp.where(mine, dest_all % PD, 0), axis=-1, keepdims=True)
    slot_v[...] = jnp.broadcast_to(slots, (ND, EMB))
    slot_copy = pltpu.make_async_copy(slot_v, slot_s, sem_slot)
    slot_copy.start()

    step3()

    @pl.loop(0, PD)
    def _(p):
        fetch_t(p).wait()
        xq[pl.ds(pl.multiple_of(p * QW, 16), QW), :] = ts_v[p, 0:QW, :]

    step4()
    got("s_q_zm", "s_q_zp", "s_q_x", "s_q_xzm", "s_q_xzp", "s_q_zz", "s_q_xzz")

    @pl.loop(0, NT // 2)
    def _(h):
        w = jnp.concatenate([wq[2 * h], wq[2 * h + 1]], axis=1)
        qm[:, pl.ds(pl.multiple_of(h * 256, 256), 256)] = mm(xq[...], w).astype(BF16)

    got("s_k_zm", "s_k_zp", "s_k_x", "s_k_xzm", "s_k_xzp", "s_k_zz", "s_k_xzz")

    @pl.loop(0, TD // 256)
    def _(b):
        rows = pl.ds(pl.multiple_of(b * 256, 256), 256)
        w = jnp.concatenate([wk[h, rows, :] for h in range(NT)], axis=1)
        tm[:, rows] = mm(qm[...], w, NT_DIMS).astype(BF16)

    @pl.loop(0, PD // 2)
    def _(i):
        for p in (2 * i, 2 * i + 1):
            t_rows = tm[pl.ds(pl.multiple_of(p * QW, 16), QW), :]
            raw = mm(t_rows, ts_v[p, QW : QW + LP, :], NT_DIMS) * (1.0 / 32.0)
            maps[p, :, 0:LP] = raw.astype(BF16)

    slot_copy.wait()
    mcopies = []
    for d in range(1, ND):
        stage[d] = maps[slot_s[(dp + d) % ND, 0]]
    rmaps[dp] = maps[slot_s[dp, 0]]
    for d in range(1, ND):
        c = rcopy(stage.at[d], rmaps.at[dp], sem_d, d - 1, ((dp + d) % ND, tn))
        go(c)
        mcopies.append(c)
    for c in qcopies + mcopies:
        c.wait_recv()

    def score(j, loss):
        r = jnp.int32(0)
        for k in range(PD):
            r = jnp.maximum(r, jnp.where(dest_s[k] // (PD * NT) == j, k, 0))
        q = qbuf[j]
        u = u16[r]
        lg = mm(q, u, NT_DIMS) * (1.0 / SHARP)
        t = CAP * jnp.tanh(rmaps[j][:, 0:LP].astype(F32) * (1.0 / CAP))
        valid = lax.broadcasted_iota(jnp.int32, (QW, LP), 1) < len_s[r]
        s_exp = jnp.where(valid, jnp.exp(lg), 0.0)
        s_tot = jnp.sum(s_exp, axis=-1, keepdims=True)
        s_prob = s_exp / s_tot
        t_exp = jnp.where(valid, jnp.exp(t), 0.0)
        t_tot = jnp.sum(t_exp, axis=-1, keepdims=True)
        t_prob = t_exp / t_tot
        log_ratio = (t - jnp.log(t_tot)) - (lg - jnp.log(s_tot))
        loss = loss + jnp.sum(
            jnp.where(valid, t_prob * log_ratio, 0.0), axis=-1, keepdims=True
        )
        cg = ((s_prob - t_prob) * (1.0 / (QW * SHARP))).astype(BF16)
        ug[j] = mm(cg, q, TN_DIMS).astype(BF16)
        qgs[j, 0:QW, :] = mm(cg, u)
        return loss

    def score2(i, loss):
        return score(2 * i + 1, score(2 * i, loss))

    loss = lax.fori_loop(0, PD // 2, score2, jnp.zeros((QW, 1), F32))
    loss_row = jnp.broadcast_to(jnp.sum(loss, axis=0, keepdims=True), (8, EMB))

    @pl.loop(0, ND)
    def _(j):
        qgs[j, QW : QW + 8, :] = loss_row

    qgr[dp] = qgs[dp]
    gcopies = []
    for d in range(1, ND):
        peer = (dp + d) % ND
        c = rcopy(qgs.at[peer], qgr.at[dp], sem_e, d - 1, (peer, tn))
        go(c)
        gcopies.append(c)

    pgm = mm_exact(gain[...], proj[...].astype(F32)) * (1.0 / D)
    pb = mm_exact(bias[...], proj[...].astype(F32))

    def backward(ps, cs):
        for p in ps:
            row = pl.ds(pl.multiple_of(p * ROW, 16), LP)
            u = ug[dest_s[p] // (PD * NT)].astype(F32)
            e, il = e_s[row, :], il_s[row, :]
            d = e * il
            eg = ((u - d * jnp.sum(d * u, axis=-1, keepdims=True)) * il).astype(BF16)
            ef = eg.astype(F32)
            cs = cs + jnp.sum(ef, axis=0, keepdims=True)
            m1 = jnp.sum(ef * pgm, axis=-1, keepdims=True)
            m2 = jnp.sum(ef * (e - pb), axis=-1, keepdims=True) * (1.0 / D)
            n = mm(eg, proj[...], NT_DIMS) * gain[...]
            sg = inv_s[row, :] * (n - m1 - n2d[row, :].astype(F32) * m2)
            sg2d[row, :] = sg.astype(BF16)
            ee_s[row, :] = eg
        return cs

    cs = lax.fori_loop(
        0, PD // 2, lambda i, cs: backward([2 * i, 2 * i + 1], cs), jnp.zeros((1, EMB), F32)
    )
    cs_s[...] = jnp.broadcast_to(cs, (8, EMB))

    for c in gcopies:
        c.wait_recv()
    total = qgr[0]
    for j in range(1, ND):
        total = total + qgr[j]
    ltb[tn] = total[QW : QW + 8, :]
    lcopies = []
    for d in range(1, NT):
        c = rcopy(ltb.at[tn], ltb.at[tn], sem_l, d - 1, (dp, (tn + d) % NT))
        go(c)
        lcopies.append(c)
    qg, qd = total[0:QW, :], qd_s[...]
    qeg = (qg - qd * jnp.sum(qd * qg, axis=-1, keepdims=True)) * qil_s[...]
    hi = qeg.astype(BF16)
    lo = (qeg - hi.astype(F32)).astype(BF16)
    pq_s[...] = mm(qs[yhi], hi, TN_DIMS) + mm(qs[yhi], lo, TN_DIMS)

    orders = (("x", "y", "z"), ("y", "z", "x"), ("z", "x", "y"))
    place = {"x": x, "y": y, "z": z}

    gcol = jnp.broadcast_to(gain[...], (8, D)).T
    bcol = jnp.broadcast_to(bias[...], (8, D)).T

    def block(b):
        lo_, hi_ = 256 * b, 256 * b + 256
        ar[b, :, 0:D] = mm(c2d[:, lo_:hi_], sg2d[...], TN_DIMS).astype(BF16)
        m = mm(n2d[:, lo_:hi_], ee_s[...], TN_DIMS)
        cs_row = cs_s[0:1, :]
        pr = proj[lo_:hi_, :].astype(F32)
        pg = gcol[lo_:hi_, 0:1] * m + bcol[lo_:hi_, 0:1] * cs_row + pq_s[lo_:hi_, :]
        ar[b, :, D : D + EMB] = pg.astype(BF16)
        gg = jnp.sum(pr * m, axis=-1, keepdims=True)
        gb = jnp.sum(pr * cs_row, axis=-1, keepdims=True)
        ln = lax.broadcasted_iota(jnp.int32, (256, EMB), 1)
        ar[b, :, D + EMB :] = jnp.where(ln == 0, gg, jnp.where(ln == 1, gb, 0.0)).astype(BF16)

    gsem = [0]
    pend = {}

    def gsend(key, src, dst, to):
        c = rcopy(src, dst, sem_g, gsem[0], to)
        gsem[0] += 1
        go(c)
        pend.setdefault(key, []).append(c)

    def gwait(key):
        for c in pend[key]:
            c.wait_recv()

    def my_rows(b):
        return pl.multiple_of(core * 128, 128), pl.multiple_of(place[orders[b][0]] * 32, 32)

    def ds(i, unit, size):
        return pl.ds(pl.multiple_of(i * unit, unit), size)

    def s0(b):
        gsend(("s0", b), ar.at[b, ds(1 - core, 128, 128)], r0.at[b], sibling)

    def s1(b):
        gwait(("s0", b))
        w1[b] = (ar[b, ds(core, 128, 128), :].astype(F32) + r0[b].astype(F32)).astype(BF16)
        a = orders[b][0]
        for d in (2, 1, 3):
            gsend(("s1", b), w1.at[b, ds((place[a] + d) % 4, 32, 32)], r1.at[b, d - 1], on_axis(a, d))

    def s2(b):
        gwait(("s1", b))
        acc = w1[b, ds(place[orders[b][0]], 32, 32), :].astype(F32)
        for d in range(3):
            acc = acc + r1[b, d].astype(F32)
        w2[b] = acc.astype(BF16)
        a = orders[b][1]
        for d in (2, 1, 3):
            gsend(("s2", b), w2.at[b, :, ds((place[a] + d) % 4, 256, 256)], r2.at[b, d - 1], on_axis(a, d))

    def s3(b):
        gwait(("s2", b))
        acc = w2[b, :, ds(place[orders[b][1]], 256, 256)].astype(F32)
        for d in range(3):
            acc = acc + r2[b, d].astype(F32)
        w3[b] = acc.astype(BF16)
        a = orders[b][2]
        for d in (2, 1, 3):
            q = (place[a] + d) % 4
            gsend(
                ("s3", b), w3.at[b, ds(q // 2, 16, 16), ds(q % 2, 128, 128)], r3.at[b, d - 1], on_axis(a, d)
            )

    def spot(b, level):
        p1, p2, p3 = (place[a] for a in orders[b])
        row, rows, col, cols = core * 128, 128, 0, 1024
        if level >= 1:
            row, rows = row + p1 * 32, 32
        if level >= 2:
            col, cols = p2 * 256, 256
        if level >= 3:
            row, rows, col, cols = row + (p3 // 2) * 16, 16, col + (p3 % 2) * 128, 128
        return pl.ds(pl.multiple_of(row, rows), rows), pl.ds(pl.multiple_of(col, min(cols, 1024)), cols)

    def g3(b):
        gwait(("s3", b))
        q = place[orders[b][2]]
        acc = w3[b, ds(q // 2, 16, 16), ds(q % 2, 128, 128)].astype(F32)
        for d in range(3):
            acc = acc + r3[b, d].astype(F32)
        i, k = spot(b, 3)
        res[b, i, k] = acc.astype(BF16)
        for d in (2, 1, 3):
            gsend(("g3", b), res.at[b, i, k], res.at[b, i, k], on_axis(orders[b][2], d))

    def g2(b):
        gwait(("g3", b))
        i, k = spot(b, 2)
        for d in (2, 1, 3):
            gsend(("g2", b), res.at[b, i, k], res.at[b, i, k], on_axis(orders[b][1], d))

    def g1(b):
        gwait(("g2", b))
        i, _ = spot(b, 1)
        for d in (2, 1, 3):
            gsend(("g1", b), res.at[b, i], res.at[b, i], on_axis(orders[b][0], d))

    def g0(b):
        gwait(("g1", b))
        i, _ = spot(b, 0)
        gsend(("g0", b), res.at[b, i], res.at[b, i], sibling)

    def out(b):
        gwait(("g0", b))
        lo_, hi_ = 256 * b, 256 * b + 256
        v = res[b]
        res_o[lo_:hi_, :] = v[:, 0 : D + EMB]
        tr = v[:, D + EMB :].astype(F32).T
        gb_o[:, lo_:hi_] = tr[0:8, :]

    stages = (s0, s1, s2, s3, g3, g2, g1, g0, out)

    def out_copy(p):
        return pltpu.make_async_copy(ctx_v.at[p], gc_h.at[p], sem_out.at[p])

    def context_grad(i):
        @pl.loop(i, i + 1)
        def _(k):
            for p in (2 * k, 2 * k + 1):
                row = pl.ds(pl.multiple_of(p * ROW, 16), LP)
                ctx_v[p] = mm(sg2d[row, :], wo[...], NT_DIMS).astype(BF16)
                out_copy(p).start()

    chunk = 0
    for tick in range(len(stages) + 2):
        for b in range(3):
            k = tick - b
            if k == 0:
                block(b)
            if 0 <= k < len(stages):
                stages[k](b)
        if tick >= 2 and chunk < PD // 2:
            context_grad(chunk)
            chunk += 1

    for c in lcopies:
        c.wait_recv()
    loss_all = ltb[0]
    for t_ in range(1, NT):
        loss_all = loss_all + ltb[t_]
    loss_o[...] = loss_all * (1.0 / (PD * ND * NT * QW))

    @pl.loop(0, PD)
    def _(p):
        out_copy(p).wait()

    for c in started:
        c.wait_send()


def local(
    context, stream, out_weight, gain, bias, proj_weight, query_states, passage_len, passage_dest,
    teacher_states, teacher_query, teacher_key,
):
    dest_v = jnp.pad(passage_dest, (0, EMB - PD))[None, :]
    smem = pl.BlockSpec(memory_space=pltpu.SMEM)
    vmem = pl.BlockSpec(memory_space=pltpu.VMEM)
    hbm = pl.BlockSpec(memory_space=pl.ANY)
    v = pltpu.VMEM
    dma = pltpu.SemaphoreType.DMA
    scratch = [
        v((PD, LP, D), BF16), v((PD, LP, D), BF16), v((PD, QW + LP, TD), BF16),
        v((FLAT, D), BF16), v((FLAT, D), BF16), v((FLAT, D), BF16),
        v((FLAT, EMB), F32), v((FLAT, EMB), BF16), v((FLAT, 1), F32), v((FLAT, 1), F32),
        v((PD, LP, EMB), BF16), v((PD, LP, EMB), BF16),
        v((NT, TD, EMB), BF16), v((NT, TD, EMB), BF16),
        v((PD, QW, 256), BF16), v((ND, QW, 256), BF16), v((ND, QW, 256), BF16),
        v((ND, QW, EMB), BF16), v((QW, EMB), F32), v((QW, EMB), F32),
        v((ND, 1, EMB), jnp.int32), v((ND, EMB), jnp.int32), pltpu.SMEM((ND, EMB), jnp.int32),
        v((ND, QW + 8, EMB), F32), v((ND, QW + 8, EMB), F32), v((NT, 8, EMB), F32),
        v((D, EMB), F32), v((8, EMB), F32),
        v((PD * QW, TD), BF16), v((PD * QW, TD), BF16), v((PD * QW, TD), BF16),
        v((3, 256, 1024), BF16), v((3, 128, 1024), BF16), v((3, 128, 1024), BF16),
        v((3, 3, 32, 1024), BF16), v((3, 32, 1024), BF16), v((3, 3, 32, 256), BF16),
        v((3, 32, 256), BF16), v((3, 3, 16, 128), BF16), v((3, 256, 1024), BF16),
        dma((2, PD)), dma((PD,)), dma((2,)), dma, dma((PD,)),
        dma((2, ND - 1)), dma((2, 40)), dma((2, ND - 1)), dma((2, ND - 1)), dma((2, ND - 1)),
        dma((2, NT - 1)), dma((2, 60)),
    ]
    grad_context, res, gb, loss = pl.pallas_call(
        kernel,
        out_shape=(
            jax.ShapeDtypeStruct((PD, LP, D), BF16),
            jax.ShapeDtypeStruct((D, D + EMB), BF16),
            jax.ShapeDtypeStruct((8, D), F32),
            jax.ShapeDtypeStruct((8, EMB), F32),
        ),
        in_specs=[smem, smem, hbm, hbm, hbm, vmem, vmem, vmem, vmem, vmem, vmem, hbm, hbm],
        out_specs=(hbm, vmem, vmem, vmem),
        scratch_shapes=scratch,
        compiler_params=pltpu.CompilerParams(
            collective_id=0, has_side_effects=True, vmem_limit_bytes=67043328
        ),
        name="distill",
    )(
        passage_dest, passage_len, context, stream, teacher_states, out_weight, gain[None, :],
        bias[None, :], proj_weight, query_states, dest_v, teacher_query, teacher_key,
    )
    return (
        loss[0, 0], res[:, :D].astype(F32), res[:, D:].astype(F32), gb[0], gb[1], grad_context,
    )


def solution(mesh):
    return jax.shard_map(
        local,
        mesh=mesh,
        in_specs=(
            P(("dp", "tensor"), None, None),
            P(("dp", "tensor"), None, None),
            P(),
            P(),
            P(),
            P(),
            P("dp", None, None),
            P(("dp", "tensor")),
            P(("dp", "tensor")),
            P(("dp", "tensor"), None, None),
            P(None, "tensor"),
            P(None, "tensor"),
        ),
        out_specs=(P(), P(), P(), P(), P(), P(("dp", "tensor"), None, None)),
        check_vma=False,
    )
```

time: 928 us -> 135 us (0.15)
  waiting for transfers between devices: 656 us -> 0 us
  matrix products: 118 us -> 0 us
  Pallas kernels: 0 us -> 101 us
  blocking collectives: 65.1 us -> 0 us
  starting transfers between devices: 28.3 us -> 0 us
  between operations: 16.1 us -> 0.65 us
  other arithmetic: 17 us -> 4.54 us
    all_gather x1 -> x0, waiting for transfers between devices: 536 us -> none  [local(): piece = lax.all_gather(teacher_states, 'tensor', axis=0, tiled=True)]
    dot_general x16 -> x0, matrix products: 118 us -> none  [the longest x1 23.3 us: local(): jnp.einsum('pte,de->ptd', embed_grad, proj_weight, preferred_element_type...]
    pallas_call x0 -> x1, Pallas kernels: none -> 101 us  [local(): pl.pallas_call(kernel, out_shape=(jax.ShapeDtypeStruct((PD, LP, D), BF16)...]
    psum x1 -> x0, waiting for transfers between devices: 75.7 us -> none  [local(): lax.psum((loss_part, wo_grad, proj_grad, gain_grad, bias_grad), ('dp', 't...]
    psum x1 -> x0, blocking collectives: 65.1 us -> none  [local(): lax.psum((loss_part, wo_grad, proj_grad, gain_grad, bias_grad), ('dp', 't...]
    all_to_all x3 -> x0, starting transfers between devices: 28.2 us -> none  [the longest x1 15.8 us: local(): lax.all_to_all(send_units, 'dp', split_axis=0, concat_axis=0, tiled=True)]
    reduce_scatter x1 -> x0, waiting for transfers between devices: 24.6 us -> none  [local(): lax.psum_scatter(partials, 'tensor', scatter_dimension=0, tiled=True)]
    all_to_all x3 -> x0, waiting for transfers between devices: 18.8 us -> none  [the longest x1 10.2 us: local(): lax.all_to_all(send_units, 'dp', split_axis=0, concat_axis=0, tiled=True)]
  transfers between devices with their start and end apart: 6 -> 0, of which waited for: 5 -> 0; matrix products, arithmetic and copies ran while one was open for 4% -> 0% of each run, Pallas kernels for 0% -> 0%
where the time goes in v1:
time: 135 us
  Pallas kernels  101 us (75%)
  local copies, waits for them, and re-layouts  28.1 us (21%)
  other arithmetic  4.54 us (3%)
    pallas_call x1, Pallas kernels, local(): pl.pallas_call(kernel, out_shape=(jax.ShapeDtypeStruct((PD, LP, D), BF16)...  101 us
    unnamed x10, local copies, waits for them, and re-layouts  21.8 us
    convert_element_type x1, other arithmetic, local(): res[:, :D].astype(F32)  2.85 us

profile of v1, /device:TPU:1, one launch (start us, length us, event | category | flops | bytes accessed | tf_op | source)
XLA Modules:
  0.0 134.7 jit_solution(3843483359051361159)
XLA Ops:
  0.6 1.2 pad_bitcast_fusion.dest_v
  1.8 1.3 broadcast_in_dim.9.gain
  3.1 1.3 broadcast_in_dim.10.bias
  4.3 0.0 copy-start
  4.3 0.0 slice-start
  4.3 6.0 %copy.18.ctx_h = bf16[16,180,768]{2,1,0:T(8,128)(2,1)} copy(bf16[16,180,768]{2,0,1:T(8,128)(2,1)} %param.12) | data formatting | bytes 8847360 | tf_op args[0]
  10.4 0.0 copy-done
  10.4 0.0 slice-start.1
  10.4 3.7 %copy.19.str_h = bf16[16,180,768]{2,1,0:T(8,128)(2,1)} copy(bf16[16,180,768]{2,0,1:T(8,128)(2,1)S(1)} %copy-done) | data formatting | bytes 8847360 | tf_op args[1]
  14.1 0.0 slice-done
  14.1 0.0 slice-done.1
  14.1 6.8 %copy.20.ts_h = bf16[16,212,1024]{2,1,0:T(8,128)(2,1)} copy(bf16[16,212,1024]{2,0,1:T(8,128)(2,1)S(1)} %bitcast.4) | data formatting | bytes 13893632 | tf_op args[9]
  20.9 101.4 %distill.1 = (bf16[16,180,768]{2,1,0:T(8,128)(2,1)}, bf16[768,896]{1,0:T(8,128)(2,1)}, f32[8,768]{1,0:T(8,128)}, f32[8,128]{1,0:T(8,128)}) custom-call(s32[16]{0:T(128)} %dest_s.1, s32[16]{0:T(128)} %len_s.1, bf16[16,180,768]{2,1,0:T(8,128)(2,1)} %copy.18.ctx_h, bf16[16,180,768]{2,1,0:T(8,128)(2,1)} %copy.19.str_h, bf16[16,212,1024]{2,1,0:T(8,128)(2,1)} %copy.20.ts_h, ...), custom_call_target="tpu_custom_call" | custom-call | tf_op jit(solution)/shard_map/distill/pallas_call | solution.py:573
  122.3 1.2 slice.15
  123.5 1.4 %slice_reduce_fusion = (f32[768]{0:T(1024)}, f32[768]{0:T(1024)}) fusion(f32[8,768]{1,0:T(8,128)} %get-tuple-element.12), kind=kLoop, calls=%fused_computation.2 | loop fusion | bytes 12288 | tf_op jit(solution)/shard_map/slice | solution.py:593
  124.9 1.7 %slice_convert_fusion.1 = f32[768,128]{1,0:T(8,128)} fusion(bf16[768,896]{1,0:T(8,128)(2,1)} %get-tuple-element.11), kind=kLoop, calls=%fused_computation.1 | loop fusion | flops 98304 | bytes 589824 | tf_op jit(solution)/shard_map/convert_element_type | solution.py:593
  126.6 2.8 %slice_convert_fusion = f32[768,768]{1,0:T(8,128)} fusion(bf16[768,896]{1,0:T(8,128)(2,1)} %get-tuple-element.11), kind=kLoop, calls=%fused_computation | loop fusion | flops 589824 | bytes 3538944 | tf_op jit(solution)/shard_map/convert_element_type | solution.py:593
  129.4 5.2 %copy.21 = bf16[16,180,768]{2,0,1:T(8,128)(2,1)} copy(bf16[16,180,768]{2,1,0:T(8,128)(2,1)} %get-tuple-element.19) | data formatting | bytes 8847360
  (1 shorter events, 0.0 us)
Async XLA Ops:
  4.3 6.0 %copy-start = (bf16[16,180,768]{2,0,1:T(8,128)(2,1)S(1)}, bf16[16,180,768]{2,0,1:T(8,128)(2,1)}, u32[]{:S(2)}) copy-start(bf16[16,180,768]{2,0,1:T(8,128)(2,1)} %param.13) | copy-start | bytes 13271044
  4.3 9.7 %slice-start = ((s8[6946816]{0:T(1024)(128)(4,1)}), s8[4194304]{0:T(1024)(128)(4,1)S(1)}, s32[]{:S(2)}) async-start(s8[6946816]{0:T(1024)(128)(4,1)} %bitcast.3), calls=%async_computation | async-start | bytes 8388608
  10.4 3.7 %slice-start.1 = ((s8[6946816]{0:T(1024)(128)(4,1)}), s8[2752512]{0:T(1024)(128)(4,1)S(1)}, s32[]{:S(2)}) async-start(s8[6946816]{0:T(1024)(128)(4,1)} %bitcast.3), calls=%async_computation.1 | async-start | bytes 5505024

commit v2 on v1

v2 whole, which is shorter than its diff:
```python
import jax
import jax.numpy as jnp
from jax import lax
from jax.experimental import pallas as pl
from jax.experimental.pallas import tpu as pltpu
from jax.sharding import PartitionSpec as P

MESH = pl.DeviceIdType.MESH
F32, BF16 = jnp.float32, jnp.bfloat16
EPS = 1e-06
SHARP = 0.05
CAP = 10.0

PD = 16
LP = 180
FLAT = PD * LP
CH = 288
SUB = 144
NCH = FLAT // CH
D = 768
EMB = 128
TD = 1024
QW = 32
ND, NT = 16, 8
NN = (((1,), (0,)), ((), ()))
NT_DIMS = (((1,), (1,)), ((), ()))
TN_DIMS = (((0,), (0,)), ((), ()))


def mm(a, b, dims=NN):
    return lax.dot_general(a, b, dims, preferred_element_type=F32)


def mm_exact(a, b):
    return lax.dot_general(
        a, b, NN, precision=lax.Precision.HIGHEST, preferred_element_type=F32
    )


class Copy:
    def __init__(self, copy):
        self.copy = copy
        self.received = False
        copy.start()

    def recv(self):
        if not self.received:
            self.copy.wait_recv()
        self.received = True


def kernel(
    dest_s, len_s, ctx_h, str_h, ts_h, wo, gain_r, bias_r, proj, qs, wq_h, wk_h,
    gc_h, res_o, gb_o,
    ctx_v, str_v, ts_v, n2d, e_s, d_s, ug_s, ee_s, inv_s, il_s,
    wq, wk, rawt, maps, stage, rmaps, qbuf, qd_s, qil_s, dinfo, slot_v, slot_s, qtmp, u16, prob, logp, qgs, qgr, ltb,
    pq_s, cs_s, qm, tmf, tm, ar, r0, w1, r1, w2, r2, res,
    sem_in, sem_ts, sem_w, sem_slot, sem_out, sem_a, sem_b, sem_c, sem_d, sem_e, sem_l, sem_g,
):
    sg2d = str_v
    dp, tn = lax.axis_index("dp"), lax.axis_index("tensor")
    ylo, x, core = dp // 8, (dp // 2) % 4, dp % 2
    yhi, z = tn // 4, tn % 4
    y = yhi * 2 + ylo
    gain = gain_r[...].reshape(1, D)
    bias = bias_r[...].reshape(1, D)

    def dev(y_, x_, core_, z_):
        return ((y_ % 2) * 8 + x_ * 2 + core_, (y_ // 2) * 4 + z_)

    def on_axis(axis, d):
        if axis == "x":
            return dev(y, (x + d) % 4, core, z)
        if axis == "y":
            return dev((y + d) % 4, x, core, z)
        return dev(y, x, core, (z + d) % 4)

    sibling = dev(y, x, 1 - core, z)
    cross = ((dp + 8) % ND, (tn + 4) % NT)

    def chunk(i):
        return pl.ds(pl.multiple_of(i * CH, CH), CH)

    def subs(i):
        return [pl.ds(pl.multiple_of(i * CH + k * SUB, SUB), SUB) for k in range(CH // SUB)]

    def fetch(i):
        return (
            pltpu.make_async_copy(ctx_h.at[chunk(i)], ctx_v.at[chunk(i)], sem_in.at[0, i]),
            pltpu.make_async_copy(str_h.at[chunk(i)], str_v.at[chunk(i)], sem_in.at[1, i]),
        )

    def t_rows(i):
        return pl.ds(pl.multiple_of(i * 848, 16), 848)

    def fetch_t(i):
        return pltpu.make_async_copy(ts_h.at[t_rows(i)], ts_v.at[t_rows(i)], sem_ts.at[i])

    @pl.loop(0, NCH)
    def _(i):
        for c in fetch(i):
            c.start()

    own_w = [
        pltpu.make_async_copy(wq_h, wq.at[tn], sem_w.at[0]),
        pltpu.make_async_copy(wk_h, wk.at[tn], sem_w.at[1]),
    ]
    for c in own_w:
        c.start()

    peers = [
        dev((y + dy) % 4, (x + dx) % 4, core, (z + dz) % 4)
        for dy in range(4) for dx in range(4) for dz in range(4)
        if (dy, dx, dz).count(0) in (1, 2)
    ]
    peers += [dev((dp_y + yhi * 2), (x + dx) % 4, 1 - core, z) for dp_y in (ylo, 1 - ylo) for dx in range(4)]
    barrier = pltpu.get_barrier_semaphore()
    for peer in peers:
        pl.semaphore_signal(barrier, inc=1, device_id=peer, device_id_type=MESH)

    q_in = qs[yhi]
    q_emb = mm(q_in, proj[...])
    q_il = lax.rsqrt(jnp.sum(q_emb * q_emb, axis=-1, keepdims=True) + EPS)
    q_dir = q_emb * q_il
    qd_s[...] = q_dir
    qil_s[...] = jnp.broadcast_to(q_il, (QW, EMB))
    qbuf[dp] = q_dir.astype(BF16)
    lane1 = lax.broadcasted_iota(jnp.int32, (1, EMB), 1)
    dest_row = jnp.zeros((1, EMB), jnp.int32)
    for k in range(PD):
        dest_row = jnp.where(lane1 == k, dest_s[k], dest_row)
    dinfo[dp] = dest_row
    maps[...] = jnp.zeros((PD, QW, 256), BF16)

    for c in own_w:
        c.wait()
    pl.semaphore_wait(barrier, len(peers))

    started = []

    def rcopy(src, dst, sem, k, to):
        c = Copy(
            pltpu.make_async_remote_copy(
                src_ref=src, dst_ref=dst, send_sem=sem.at[0, k], recv_sem=sem.at[1, k],
                device_id=to, device_id_type=MESH,
            )
        )
        started.append(c)
        return c

    def finish():
        for c in started:
            c.recv()
        for c in started:
            c.copy.wait_send()

    def send_all(buf, sem):
        out = []
        for d in range(1, ND):
            c = rcopy(buf.at[dp], buf.at[dp], sem, d - 1, ((dp + d) % ND, tn))
            out.append(c)
        return out

    dcopies = send_all(dinfo, sem_a)
    half = TD // 2
    base = core * half
    wcopies = {}
    counter = [0]

    def rows_of(part):
        if part == "all":
            return base, half
        if part == "hi":
            return base, half // 2
        return base + half // 2, half // 2

    def wsend(name, buf, t_, part, to):
        start, size = rows_of(part)
        view = buf.at[t_, pl.ds(pl.multiple_of(start, 16), size)]
        c = rcopy(view, view, sem_b, counter[0], to)
        counter[0] += 1
        wcopies[name] = c

    zp, zm = on_axis("z", 1), on_axis("z", 3)
    t_zm, t_zp, t_zz = yhi * 4 + (z + 3) % 4, yhi * 4 + (z + 1) % 4, yhi * 4 + (z + 2) % 4

    def flip(t_):
        return (t_ + 4) % NT

    wsend("q_x", wq, tn, "all", cross)
    wsend("q_zp", wq, tn, "all", zp)
    wsend("q_zm", wq, tn, "all", zm)
    wsend("k_zp", wk, tn, "all", zp)
    wsend("k_zm", wk, tn, "all", zm)
    wsend("k_x", wk, tn, "all", cross)
    qcopies = send_all(qbuf, sem_c)

    def got(*names):
        for n in names:
            wcopies[n].recv()

    def step2q():
        got("q_zp", "q_zm", "q_x")
        wsend("q_x_zp", wq, flip(tn), "all", zp)
        wsend("q_x_zm", wq, flip(tn), "all", zm)
        wsend("q_zz_p", wq, t_zm, "hi", zp)
        wsend("q_zz_m", wq, t_zp, "lo", zm)
        wsend("s_q_zm", wq, t_zm, "all", sibling)
        wsend("s_q_zp", wq, t_zp, "all", sibling)
        wsend("s_q_x", wq, flip(tn), "all", sibling)

    def step2k():
        got("k_zp", "k_zm", "k_x")
        wsend("k_zm_x", wk, t_zm, "all", cross)
        wsend("k_zp_x", wk, t_zp, "all", cross)
        wsend("k_zz_p", wk, t_zm, "hi", zp)
        wsend("k_zz_m", wk, t_zp, "lo", zm)
        wsend("s_k_zm", wk, t_zm, "all", sibling)
        wsend("s_k_zp", wk, t_zp, "all", sibling)
        wsend("s_k_x", wk, flip(tn), "all", sibling)

    def step3q():
        got("q_x_zp", "q_x_zm")
        wsend("q_xzz_p", wq, flip(t_zm), "hi", zp)
        wsend("q_xzz_m", wq, flip(t_zp), "lo", zm)
        wsend("s_q_xzm", wq, flip(t_zm), "all", sibling)
        wsend("s_q_xzp", wq, flip(t_zp), "all", sibling)
        got("q_zz_p", "q_zz_m")
        wsend("s_q_zz", wq, t_zz, "all", sibling)

    def step3k():
        got("k_zz_p", "k_zz_m")
        wsend("k_zz_x", wk, t_zz, "all", cross)
        wsend("s_k_zz", wk, t_zz, "all", sibling)

    def step4():
        got("q_xzz_p", "q_xzz_m")
        wsend("s_q_xzz", wq, flip(t_zz), "all", sibling)
        got("k_zm_x", "k_zp_x")
        wsend("s_k_xzm", wk, flip(t_zm), "all", sibling)
        wsend("s_k_xzp", wk, flip(t_zp), "all", sibling)

    def step5():
        got("k_zz_x")
        wsend("s_k_xzz", wk, flip(t_zz), "all", sibling)

    def forward(i):
        for c in fetch(i):
            c.wait()
        rows = subs(i)
        sums = [mm(ctx_v[r, :], wo[...]) for r in rows]
        for r, s in zip(rows, sums):
            s = s + str_v[r, :].astype(F32)
            c = s - jnp.mean(s, axis=-1, keepdims=True)
            inv = lax.rsqrt(jnp.mean(c * c, axis=-1, keepdims=True) + EPS)
            n = c * inv
            h = (n * gain + bias).astype(BF16)
            e = mm(h, proj[...])
            il = lax.rsqrt(jnp.sum(e * e, axis=-1, keepdims=True) + EPS)
            n2d[r, :] = n.astype(BF16)
            inv_s[r, :] = inv
            e_s[r, :] = e
            il_s[r, :] = il
            d_s[r, :] = e * il

    def forward_loop(lo, hi):
        @pl.loop(lo, hi)
        def _(i):
            forward(i)

    @pl.loop(0, 4)
    def _(i):
        fetch_t(i).start()

    forward_loop(0, 2)
    step2q()
    forward_loop(2, 4)
    step2k()
    forward_loop(4, 6)
    step3q()
    forward_loop(6, 7)
    step3k()
    forward_loop(7, 8)
    step4()
    forward_loop(8, NCH)

    for c in dcopies:
        c.recv()
    dest_all = dinfo[:, 0, :]
    lane = lax.broadcasted_iota(jnp.int32, (ND, EMB), 1)
    mine = jnp.logical_and((dest_all // (PD * NT)) == dp, lane < PD)
    slots = jnp.max(jnp.where(mine, dest_all % PD, 0), axis=-1, keepdims=True)
    slot_v[...] = jnp.broadcast_to(slots, (ND, EMB))
    slot_copy = pltpu.make_async_copy(slot_v, slot_s, sem_slot)
    slot_copy.start()

    @pl.loop(0, 4)
    def _(i):
        fetch_t(i).wait()

    got("s_q_zm", "s_q_zp", "s_q_x", "s_q_xzm", "s_q_xzp", "s_q_zz", "s_q_xzz")

    @pl.loop(0, NT // 2)
    def _(h):
        w = jnp.concatenate([wq[2 * h], wq[2 * h + 1]], axis=1)
        qm[:, pl.ds(pl.multiple_of(h * 256, 256), 256)] = mm(ts_v[0 : PD * QW, :], w).astype(BF16)

    step5()
    got("s_k_zm", "s_k_zp", "s_k_x", "s_k_xzm", "s_k_xzp", "s_k_zz", "s_k_xzz")

    @pl.loop(0, TD // 256)
    def _(b):
        rows = pl.ds(pl.multiple_of(b * 256, 256), 256)
        w = jnp.concatenate([wk[h, rows, :] for h in range(NT)], axis=1)
        t = mm(qm[...], w, NT_DIMS)
        tmf[2 * b] = t[:, 0:128]
        tmf[2 * b + 1] = t[:, 128:256]

    @pl.loop(0, PD)
    def _(p):
        for k in range(TD // 128):
            part = tmf.at[k][pl.ds(p, QW, stride=PD), :]
            tm[pl.ds(pl.multiple_of(p * QW, QW), QW), 128 * k : 128 * k + 128] = part.astype(BF16)

    @pl.loop(0, NCH)
    def _(i):
        keys = ts_v[pl.ds(pl.multiple_of(PD * QW + i * CH, 16), CH), :]
        full = mm(keys, tm[...], NT_DIMS)
        own = lax.broadcasted_iota(jnp.int32, (CH, PD * QW), 0) % PD
        col = lax.broadcasted_iota(jnp.int32, (CH, PD * QW), 1) // QW
        full = jnp.where(own == col, full, 0.0)
        part = full[:, 0:128] + full[:, 128:256] + full[:, 256:384] + full[:, 384:512]
        part = part + pltpu.roll(part, 64, 1)
        part = part + pltpu.roll(part, 32, 1)
        rawt[chunk(i), :] = part * (1.0 / 32.0)

    @pl.loop(0, PD)
    def _(p):
        pair = rawt[pl.ds(p, LP, stride=PD), :]
        maps[p, :, 0:LP] = pair.T[0:QW, :].astype(BF16)

    slot_copy.wait()
    mcopies = []
    for d in range(1, ND):
        stage[d] = maps[slot_s[(dp + d) % ND, 0]]
    rmaps[dp] = maps[slot_s[dp, 0]]
    for d in range(1, ND):
        c = rcopy(stage.at[d], rmaps.at[dp], sem_d, d - 1, ((dp + d) % ND, tn))
        mcopies.append(c)
    for c in qcopies:
        c.recv()

    def student(p):
        u = d_s[pl.ds(p, LP, stride=PD), :].astype(BF16)
        lg = mm(qbuf[dest_s[p] // (PD * NT)], u, NT_DIMS) * (1.0 / SHARP)
        valid = lax.broadcasted_iota(jnp.int32, (QW, LP), 1) < len_s[p]
        s_exp = jnp.where(valid, jnp.exp(lg), 0.0)
        s_tot = jnp.sum(s_exp, axis=-1, keepdims=True)
        u16[p] = u
        prob[p, :, 0:LP] = s_exp / s_tot
        logp[p, :, 0:LP] = lg - jnp.log(s_tot)

    @pl.loop(0, PD // 2)
    def _(i):
        student(2 * i)
        student(2 * i + 1)

    for c in mcopies:
        c.recv()

    def score(p, loss):
        j = dest_s[p] // (PD * NT)
        t = CAP * jnp.tanh(rmaps[j][:, 0:LP].astype(F32) * (1.0 / CAP))
        valid = lax.broadcasted_iota(jnp.int32, (QW, LP), 1) < len_s[p]
        t_exp = jnp.where(valid, jnp.exp(t), 0.0)
        t_tot = jnp.sum(t_exp, axis=-1, keepdims=True)
        t_prob = t_exp / t_tot
        log_ratio = (t - jnp.log(t_tot)) - logp[p, :, 0:LP]
        loss = loss + jnp.sum(
            jnp.where(valid, t_prob * log_ratio, 0.0), axis=-1, keepdims=True
        )
        cg = ((prob[p, :, 0:LP] - t_prob) * (1.0 / (QW * SHARP))).astype(BF16)
        ug_s[pl.ds(p, LP, stride=PD), :] = mm(cg, qbuf[j], TN_DIMS).astype(BF16).astype(F32)
        qtmp[p] = mm(cg, u16[p])
        return loss

    def score2(i, loss):
        return score(2 * i + 1, score(2 * i, loss))

    loss = lax.fori_loop(0, PD // 2, score2, jnp.zeros((QW, 1), F32))
    loss_row = jnp.broadcast_to(jnp.sum(loss, axis=0, keepdims=True), (8, EMB))

    @pl.loop(0, ND)
    def _(j):
        r = jnp.int32(0)
        for k in range(PD):
            r = jnp.maximum(r, jnp.where(dest_s[k] // (PD * NT) == j, k, 0))
        qgs[j, 0:QW, :] = qtmp[r]
        qgs[j, QW : QW + 8, :] = loss_row

    qgr[dp] = qgs[dp]
    gcopies = []
    for d in range(1, ND):
        peer = (dp + d) % ND
        c = rcopy(qgs.at[peer], qgr.at[dp], sem_e, d - 1, (peer, tn))
        gcopies.append(c)

    pgm = mm_exact(gain, proj[...].astype(F32)) * (1.0 / D)
    pb = mm_exact(bias, proj[...].astype(F32))

    def backward(i, cs):
        for r in subs(i):
            u, e, d, il = ug_s[r, :], e_s[r, :], d_s[r, :], il_s[r, :]
            eg = ((u - d * jnp.sum(d * u, axis=-1, keepdims=True)) * il).astype(BF16)
            ef = eg.astype(F32)
            cs = cs + jnp.sum(ef, axis=0, keepdims=True)
            m1 = jnp.sum(ef * pgm, axis=-1, keepdims=True)
            m2 = jnp.sum(ef * (e - pb), axis=-1, keepdims=True) * (1.0 / D)
            n = mm(eg, proj[...], NT_DIMS) * gain
            sg = inv_s[r, :] * (n - m1 - n2d[r, :].astype(F32) * m2)
            sg2d[r, :] = sg.astype(BF16)
            ee_s[r, :] = eg
        return cs

    cs = lax.fori_loop(0, NCH, backward, jnp.zeros((1, EMB), F32))
    cs_s[...] = jnp.broadcast_to(cs, (8, EMB))

    for c in gcopies:
        c.recv()
    total = qgr[0]
    for j in range(1, ND):
        total = total + qgr[j]
    ltb[tn] = total[QW : QW + 8, :]
    lcopies = []
    for d in range(1, NT):
        c = rcopy(ltb.at[tn], ltb.at[tn], sem_l, d - 1, (dp, (tn + d) % NT))
        lcopies.append(c)
    qg, qd = total[0:QW, :], qd_s[...]
    qeg = (qg - qd * jnp.sum(qd * qg, axis=-1, keepdims=True)) * qil_s[...]
    hi = qeg.astype(BF16)
    lo = (qeg - hi.astype(F32)).astype(BF16)
    pq_s[...] = mm(qs[yhi], hi, TN_DIMS) + mm(qs[yhi], lo, TN_DIMS)

    orders = (("x", "y", "z"), ("y", "z", "x"), ("z", "x", "y"))
    place = {"x": x, "y": y, "z": z}

    gcol = jnp.broadcast_to(gain, (8, D)).T
    bcol = jnp.broadcast_to(bias, (8, D)).T

    def block(b):
        lo_, hi_ = 256 * b, 256 * b + 256
        ar[b, :, 0:D] = mm(ctx_v[:, lo_:hi_], sg2d[...], TN_DIMS).astype(BF16)
        m = mm(n2d[:, lo_:hi_], ee_s[...], TN_DIMS)
        cs_row = cs_s[0:1, :]
        pr = proj[lo_:hi_, :].astype(F32)
        pg = gcol[lo_:hi_, 0:1] * m + bcol[lo_:hi_, 0:1] * cs_row + pq_s[lo_:hi_, :]
        ar[b, :, D : D + EMB] = pg.astype(BF16)
        gg = jnp.sum(pr * m, axis=-1, keepdims=True)
        gb = jnp.sum(pr * cs_row, axis=-1, keepdims=True)
        ln = lax.broadcasted_iota(jnp.int32, (256, EMB), 1)
        ar[b, :, D + EMB :] = jnp.where(ln == 0, gg, jnp.where(ln == 1, gb, 0.0)).astype(BF16)

    gsem = [0]
    pend = {}

    def gsend(key, src, dst, to):
        c = rcopy(src, dst, sem_g, gsem[0], to)
        gsem[0] += 1
        pend.setdefault(key, []).append(c)

    def gwait(key):
        for c in pend[key]:
            c.recv()

    def my_rows(b):
        return pl.multiple_of(core * 128, 128), pl.multiple_of(place[orders[b][0]] * 32, 32)

    def ds(i, unit, size):
        return pl.ds(pl.multiple_of(i * unit, unit), size)

    def s0(b):
        gsend(("s0", b), ar.at[b, ds(1 - core, 128, 128)], r0.at[b], sibling)

    def s1(b):
        gwait(("s0", b))
        w1[b] = (ar[b, ds(core, 128, 128), :].astype(F32) + r0[b].astype(F32)).astype(BF16)
        a = orders[b][0]
        for d in (2, 1, 3):
            gsend(("s1", b), w1.at[b, ds((place[a] + d) % 4, 32, 32)], r1.at[b, d - 1], on_axis(a, d))

    def on_plane(b, d2, d3):
        at = {"x": x, "y": y, "z": z}
        for a, d in zip(orders[b][1:], (d2, d3)):
            at[a] = (at[a] + d) % 4
        return dev(at["y"], at["x"], core, at["z"]), (at[orders[b][1]], at[orders[b][2]])

    def piece(row, col, p2, p3):
        return (
            pl.ds(pl.multiple_of(row + (p3 // 2) * 16, 16), 16),
            pl.ds(pl.multiple_of(col + p2 * 256 + (p3 % 2) * 128, 128), 128),
        )

    shifts = [(d2, d3) for d2 in (2, 1, 3, 0) for d3 in (2, 1, 3, 0) if d2 or d3]

    def s2(b):
        gwait(("s1", b))
        acc = w1[b, ds(place[orders[b][0]], 32, 32), :].astype(F32)
        for d in range(3):
            acc = acc + r1[b, d].astype(F32)
        w2[b] = acc.astype(BF16)
        for k, (d2, d3) in enumerate(shifts):
            to, at = on_plane(b, d2, d3)
            i, j = piece(0, 0, *at)
            gsend(("s2", b), w2.at[b, i, j], r2.at[b, k], to)

    def spot(b):
        return core * 128 + place[orders[b][0]] * 32

    def g2(b):
        gwait(("s2", b))
        at = (place[orders[b][1]], place[orders[b][2]])
        i, j = piece(0, 0, *at)
        acc = w2[b, i, j].astype(F32)
        for k in range(len(shifts)):
            acc = acc + r2[b, k].astype(F32)
        i, j = piece(spot(b), 0, *at)
        res[b, i, j] = acc.astype(BF16)
        for d2, d3 in shifts:
            gsend(("g2", b), res.at[b, i, j], res.at[b, i, j], on_plane(b, d2, d3)[0])

    def g1(b):
        gwait(("g2", b))
        i = pl.ds(pl.multiple_of(spot(b), 32), 32)
        for d in (2, 1, 3):
            gsend(("g1", b), res.at[b, i], res.at[b, i], on_axis(orders[b][0], d))

    def g0(b):
        gwait(("g1", b))
        i = ds(core, 128, 128)
        gsend(("g0", b), res.at[b, i], res.at[b, i], sibling)

    def out(b):
        gwait(("g0", b))
        lo_, hi_ = 256 * b, 256 * b + 256
        v = res[b]
        res_o[lo_:hi_, :] = v[:, 0 : D + EMB]
        tr = v[:, D + EMB :].astype(F32).T
        gb_o[0:2, lo_:hi_] = tr[0:2, :]

    def out_copy(i):
        return pltpu.make_async_copy(ctx_v.at[chunk(i)], gc_h.at[chunk(i)], sem_out.at[i])

    def context_grad(lo, hi):
        @pl.loop(lo, hi)
        def _(i):
            for r in subs(i):
                ctx_v[r, :] = mm(sg2d[r, :], wo[...], NT_DIMS).astype(BF16)
            out_copy(i).start()

    block(0)
    s0(0)
    block(1)
    s1(0)
    s0(1)
    block(2)
    s0(2)
    s1(1)
    s2(0)
    context_grad(0, 2)
    s1(2)
    s2(1)
    context_grad(2, 5)
    g2(0)
    s2(2)
    g2(1)
    context_grad(5, 8)
    g2(2)
    g1(0)
    g1(1)
    context_grad(8, NCH)
    g1(2)
    g0(0)
    g0(1)
    out(0)
    out(1)
    g0(2)
    out(2)

    for c in lcopies:
        c.recv()
    loss_all = ltb[0]
    for t_ in range(1, NT):
        loss_all = loss_all + ltb[t_]
    gb_o[2:3, 0:EMB] = loss_all[0:1, :] * (1.0 / (PD * ND * NT * QW))

    @pl.loop(0, NCH)
    def _(i):
        out_copy(i).wait()

    finish()


def local(
    context, stream, out_weight, gain, bias, proj_weight, query_states, passage_len, passage_dest,
    teacher_states, teacher_query, teacher_key,
):
    flat = lambda a: a.transpose(1, 0, 2).reshape(-1, a.shape[2])
    smem = pl.BlockSpec(memory_space=pltpu.SMEM)
    vmem = pl.BlockSpec(memory_space=pltpu.VMEM)
    hbm = pl.BlockSpec(memory_space=pl.ANY)
    v = pltpu.VMEM
    dma = pltpu.SemaphoreType.DMA
    scratch = [
        v((FLAT, D), BF16), v((FLAT, D), BF16), v((PD * (QW + LP), TD), BF16), v((FLAT, D), BF16),
        v((FLAT, EMB), F32), v((FLAT, EMB), F32), v((FLAT, EMB), F32), v((FLAT, EMB), BF16),
        v((FLAT, 1), F32), v((FLAT, 1), F32),
        v((NT, TD, EMB), BF16), v((NT, TD, EMB), BF16), v((FLAT, EMB), F32),
        v((PD, QW, 256), BF16), v((ND, QW, 256), BF16), v((ND, QW, 256), BF16),
        v((ND, QW, EMB), BF16), v((QW, EMB), F32), v((QW, EMB), F32),
        v((ND, 1, EMB), jnp.int32), v((ND, EMB), jnp.int32), pltpu.SMEM((ND, EMB), jnp.int32),
        v((PD, QW, EMB), F32), v((PD, LP, EMB), BF16), v((PD, QW, 256), F32), v((PD, QW, 256), F32),
        v((ND, QW + 8, EMB), F32), v((ND, QW + 8, EMB), F32), v((NT, 8, EMB), F32),
        v((D, EMB), F32), v((8, EMB), F32),
        v((PD * QW, TD), BF16), v((TD // 128, PD * QW, 128), F32), v((PD * QW, TD), BF16),
        v((3, 256, 1024), BF16), v((3, 128, 1024), BF16), v((3, 128, 1024), BF16),
        v((3, 3, 32, 1024), BF16), v((3, 32, 1024), BF16), v((3, 15, 16, 128), BF16), v((3, 256, 1024), BF16),
        dma((2, NCH)), dma((4,)), dma((2,)), dma, dma((NCH,)),
        dma((2, ND - 1)), dma((2, 40)), dma((2, ND - 1)), dma((2, ND - 1)), dma((2, ND - 1)),
        dma((2, NT - 1)), dma((2, 114)),
    ]
    grad_context, res, gb = pl.pallas_call(
        kernel,
        out_shape=(
            jax.ShapeDtypeStruct((FLAT, D), BF16),
            jax.ShapeDtypeStruct((D, D + EMB), BF16),
            jax.ShapeDtypeStruct((8, D), F32),
        ),
        in_specs=[smem, smem, hbm, hbm, hbm, vmem, vmem, vmem, vmem, vmem, hbm, hbm],
        out_specs=(hbm, vmem, vmem),
        scratch_shapes=scratch,
        compiler_params=pltpu.CompilerParams(
            collective_id=0, has_side_effects=True, vmem_limit_bytes=67043328
        ),
        name="distill",
    )(
        passage_dest, passage_len, flat(context), flat(stream), flat(teacher_states), out_weight, gain,
        bias, proj_weight, query_states, teacher_query, teacher_key,
    )
    return finish_outputs(grad_context, res, gb)


def outputs_kernel(gc_h, res, gb, out_h, wo_o, proj_o, gain_o, bias_o, loss_o, buf, sem):
    def rows(i):
        return pl.ds(pl.multiple_of(i * CH, CH), CH)

    def take(i):
        return pltpu.make_async_copy(gc_h.at[rows(i)], buf.at[rows(i)], sem.at[0, i])

    def give(i):
        return pltpu.make_async_copy(buf.at[rows(i)], out_h.at[rows(i)], sem.at[1, i])

    @pl.loop(0, NCH)
    def _(i):
        take(i).start()

    for k in range(0, D, 256):
        wo_o[k : k + 256, :] = res[k : k + 256, 0:D].astype(F32)
    proj_o[...] = res[:, D:].astype(F32)
    gain_o[...] = gb[0:1, :].reshape(D)
    bias_o[...] = gb[1:2, :].reshape(D)
    loss_o[...] = gb[2:3, 0:1]

    @pl.loop(0, NCH)
    def _(i):
        take(i).wait()
        give(i).start()

    @pl.loop(0, NCH)
    def _(i):
        give(i).wait()


def finish_outputs(grad_context, res, gb):
    vmem = pl.BlockSpec(memory_space=pltpu.VMEM)
    hbm = pl.BlockSpec(memory_space=pl.ANY)
    grad_context, wo_g, proj_g, gain_g, bias_g, loss = pl.pallas_call(
        outputs_kernel,
        out_shape=(
            jax.ShapeDtypeStruct((FLAT, D), BF16),
            jax.ShapeDtypeStruct((D, D), F32),
            jax.ShapeDtypeStruct((D, EMB), F32),
            jax.ShapeDtypeStruct((D,), F32),
            jax.ShapeDtypeStruct((D,), F32),
            jax.ShapeDtypeStruct((1, 1), F32),
        ),
        in_specs=[hbm, vmem, vmem],
        out_specs=(hbm, vmem, vmem, vmem, vmem, vmem),
        scratch_shapes=[pltpu.VMEM((FLAT, D), BF16), pltpu.SemaphoreType.DMA((2, NCH))],
        name="outputs",
    )(grad_context, res, gb)
    return (
        loss.reshape(()), wo_g, proj_g, gain_g, bias_g,
        grad_context.reshape(LP, PD, D).transpose(1, 0, 2),
    )


def solution(mesh):
    return jax.shard_map(
        local,
        mesh=mesh,
        in_specs=(
            P(("dp", "tensor"), None, None),
            P(("dp", "tensor"), None, None),
            P(),
            P(),
            P(),
            P(),
            P("dp", None, None),
            P(("dp", "tensor")),
            P(("dp", "tensor")),
            P(("dp", "tensor"), None, None),
            P(None, "tensor"),
            P(None, "tensor"),
        ),
        out_specs=(P(), P(), P(), P(), P(), P(("dp", "tensor"), None, None)),
        check_vma=False,
    )
```

time: 135 us -> 106 us (0.79)
  local copies, waits for them, and re-layouts: 28.1 us -> 0 us
  other arithmetic: 4.54 us -> 0 us
  Pallas kernels: 101 us -> 105 us
    unnamed x10 -> x0, local copies, waits for them, and re-layouts: 21.8 us -> none
    convert_element_type x2 -> x0, other arithmetic: 4.54 us -> none  [the longest x1 2.85 us: local(): res[:, :D].astype(F32)]
    broadcast_in_dim x3 -> x0, local copies, waits for them, and re-layouts: 3.7 us -> none  [the longest x1 1.27 us: local(): gain[None, :]]
    pallas_call x1 -> x2, Pallas kernels: 101 us -> 105 us  [the longest x1 98.2 us: local(): pl.pallas_call(kernel, out_shape=(jax.ShapeDtypeStruct((FLAT, D), BF16),...]
    slice x2 -> x0, local copies, waits for them, and re-layouts: 2.62 us -> none  [the longest x1 1.43 us: local(): gb[1]]
where the time goes in v2:
time: 106 us
  Pallas kernels  105 us (99%)
    pallas_call x1, Pallas kernels, local(): pl.pallas_call(kernel, out_shape=(jax.ShapeDtypeStruct((FLAT, D), BF16),...  98.2 us
    pallas_call x1, Pallas kernels, finish_outputs(): pl.pallas_call(outputs_kernel, out_shape=(jax.ShapeDtypeStruct((FLAT, D),...  6.77 us

profile of v2, /device:TPU:1, one launch (start us, length us, event | category | flops | bytes accessed | tf_op | source)
XLA Modules:
  0.0 105.8 jit_solution(12865057915403375705)
XLA Ops:
  0.6 98.2 %distill.1 = (bf16[2880,768]{1,0:T(8,128)(2,1)}, bf16[768,896]{1,0:T(8,128)(2,1)}, f32[8,768]{1,0:T(8,128)}) custom-call(s32[16]{0:T(128)} %dest_s.1, s32[16]{0:T(128)} %len_s.1, bf16[2880,768]{1,0:T(8,128)(2,1)} %bitcast.14, bf16[2880,768]{1,0:T(8,128)(2,1)} %bitcast.15, bf16[3392,1024]{1,0:T(8,128)(2,1)} %bitcast.13, bf16[768,768]{1,0:T(8,128)(2,1)} %wo.1, ...), custom_call_target="tpu_custom_call" | custom-call | tf_op jit(solution)/shard_map/distill/pallas_call | solution.py:631
  98.9 6.8 %outputs.1 = (bf16[2880,768]{1,0:T(8,128)(2,1)}, f32[768,768]{1,0:T(8,128)}, f32[768,128]{1,0:T(8,128)}, f32[768]{0:T(1024)}, f32[768]{0:T(1024)}, /*index=5*/f32[1,1]{1,0:T(1,128)}) custom-call(bf16[2880,768]{1,0:T(8,128)(2,1)} %get-tuple-element.15.gc_h, bf16[768,896]{1,0:T(8,128)(2,1)} %get-tuple-element.16.res, f32[8,768]{1,0:T(8,128)} %get-tuple-element.17.gb), custom_call_target="tpu_custom_call" | custom-call | tf_op jit(solution)/shard_map/outputs/pallas_call | solution.py:686

commit v3 on v2

--- a/solution.py
+++ b/solution.py
@@ -96,17 +96,17 @@
     def fetch_t(i):
         return pltpu.make_async_copy(ts_h.at[t_rows(i)], ts_v.at[t_rows(i)], sem_ts.at[i])
 
-    @pl.loop(0, NCH)
-    def _(i):
-        for c in fetch(i):
-            c.start()
-
     own_w = [
         pltpu.make_async_copy(wq_h, wq.at[tn], sem_w.at[0]),
         pltpu.make_async_copy(wk_h, wk.at[tn], sem_w.at[1]),
     ]
     for c in own_w:
         c.start()
+
+    @pl.loop(0, NCH)
+    def _(i):
+        for c in fetch(i):
+            c.start()
 
     peers = [
         dev((y + dy) % 4, (x + dx) % 4, core, (z + dz) % 4)
@@ -161,7 +161,6 @@
             out.append(c)
         return out
 
-    dcopies = send_all(dinfo, sem_a)
     half = TD // 2
     base = core * half
     wcopies = {}
@@ -193,6 +192,7 @@
     wsend("k_zp", wk, tn, "all", zp)
     wsend("k_zm", wk, tn, "all", zm)
     wsend("k_x", wk, tn, "all", cross)
+    dcopies = send_all(dinfo, sem_a)
     qcopies = send_all(qbuf, sem_c)
 
     def got(*names):

time: 106 us -> 106 us (level)
  no operation moved by 1% of the time
where the time goes in v3:
time: 106 us
  Pallas kernels  105 us (99%)
    pallas_call x1, Pallas kernels, local(): pl.pallas_call(kernel, out_shape=(jax.ShapeDtypeStruct((FLAT, D), BF16),...  98.3 us
    pallas_call x1, Pallas kernels, finish_outputs(): pl.pallas_call(outputs_kernel, out_shape=(jax.ShapeDtypeStruct((FLAT, D),...  6.77 us

profile of v3, /device:TPU:1, one launch (start us, length us, event | category | flops | bytes accessed | tf_op | source)
XLA Modules:
  0.0 105.9 jit_solution(8818457524980566726)
XLA Ops:
  0.6 98.3 %distill.1 = (bf16[2880,768]{1,0:T(8,128)(2,1)}, bf16[768,896]{1,0:T(8,128)(2,1)}, f32[8,768]{1,0:T(8,128)}) custom-call(s32[16]{0:T(128)} %dest_s.1, s32[16]{0:T(128)} %len_s.1, bf16[2880,768]{1,0:T(8,128)(2,1)} %bitcast.14, bf16[2880,768]{1,0:T(8,128)(2,1)} %bitcast.15, bf16[3392,1024]{1,0:T(8,128)(2,1)} %bitcast.13, bf16[768,768]{1,0:T(8,128)(2,1)} %wo.1, ...), custom_call_target="tpu_custom_call" | custom-call | tf_op jit(solution)/shard_map/distill/pallas_call | solution.py:631
  99.0 6.8 %outputs.1 = (bf16[2880,768]{1,0:T(8,128)(2,1)}, f32[768,768]{1,0:T(8,128)}, f32[768,128]{1,0:T(8,128)}, f32[768]{0:T(1024)}, f32[768]{0:T(1024)}, /*index=5*/f32[1,1]{1,0:T(1,128)}) custom-call(bf16[2880,768]{1,0:T(8,128)(2,1)} %get-tuple-element.15.gc_h, bf16[768,896]{1,0:T(8,128)(2,1)} %get-tuple-element.16.res, f32[8,768]{1,0:T(8,128)} %get-tuple-element.17.gb), custom_call_target="tpu_custom_call" | custom-call | tf_op jit(solution)/shard_map/outputs/pallas_call | solution.py:686
